TPU v7x, 32 devices: a whole 2x2x4 slice. The times are simulated.
32 devices in a mesh: parts: 2 (over x), seq: 16 (over z, y, core).
Axes of the slice: x: 2, y: 2, z: 4, core: 2. Of those that a mesh axis runs over, the one named last changes fastest.
Arguments:
- queries: bfloat16 [4096, 1024], P(('parts', 'seq')), parts along dimension 0, may hold values from -6 to 6
- keys: bfloat16 [4096, 1024], P(('parts', 'seq')), parts along dimension 0, may hold values from -6 to 6
- values: bfloat16 [4096, 1024], P(('parts', 'seq')), parts along dimension 0, may hold values from -6 to 6
- log_forget: float32 [8, 4096], P(None, ('parts', 'seq')), parts along dimension 1, may hold values from -5 to 0
- input_gate: float32 [8, 4096], P(None, ('parts', 'seq')), parts along dimension 1, may hold values from 0.1 to 1
- ridge: float32 [8], replicated, may hold values from 0.25 to 4
- gain: float32 [1024], replicated, may hold values from 0.25 to 1.75
- out_weight: bfloat16 [1024, 2048], P('seq'), may hold values from -0.1875 to 0.1875
Outputs:
- mixed: bfloat16 [4096, 2048], P(('parts', 'seq')), parts along dimension 0
There are 2 independent parts, one for each index of `parts`. A program takes and returns all parts, laid end to end along the dimension named above; an argument that names none is the same for every part. Nothing has to cross between parts.
All inputs are finite; a program needn't handle non-finite values. Where the computation divides by a largest or mean magnitude, that divisor is 1e-20 or more.
Results may differ from a plain program's by a relative error of at most 0.007.
Values may be sent and summed in bfloat16 or wider, within the bound.
No kernel may reach another device: no remote copies, remote signals or barrier semaphores. Data moves between devices by JAX's collectives and lax.ppermute only.
A program may use at most 192 MiB of HBM per device.

v0:
```python
import jax
import jax.numpy as jnp
from jax import lax
from jax.sharding import PartitionSpec as P

HEADS = 8
DH = 128
C = 128
NEWTON = 6
CORR = 4
highest = lax.Precision.HIGHEST


def carried_in(array, axis, join, neutral):
    place = lax.axis_index(axis)
    gathered = jax.tree.map(
        lambda a, kind: lax.all_gather(a.astype(kind), axis), array, (jnp.bfloat16, jnp.bfloat16)
    )
    state = jax.tree.map(lambda a, e: jnp.zeros_like(a) + jnp.asarray(e, a.dtype), array, neutral)

    def one(step, state):
        return join(
            state,
            jax.tree.map(
                lambda a, own: lax.dynamic_index_in_dim(a, step, 0, False).astype(own.dtype),
                gathered,
                array,
            ),
        )

    return lax.fori_loop(0, place, one, state)


def prefix(value, axis, join, neutral):
    count, mine = (lax.axis_size(axis), lax.axis_index(axis))
    pieces = jax.tree.map(lambda part: lax.all_gather(part, axis), value)
    total = jax.tree.map(
        lambda part, zero: jnp.full_like(part, 0) + jnp.asarray(zero, part.dtype), value, neutral
    )

    def step(position, total):
        longer = join(total, jax.tree.map(lambda part: part[position], pieces))
        return jax.tree.map(lambda new, old: jnp.where(position < mine, new, old), longer, total)

    return lax.fori_loop(0, count - 1, step, total)


def product(left, right):
    return jnp.matmul(left, right, precision=highest)


def unit_rows(field):
    return field * lax.rsqrt(jnp.sum(field * field, axis=-1, keepdims=True) + 1e-06)


def add_pairs(earlier, later):
    shrink = jnp.exp(later[0])[:, None, None]
    return (earlier[0] + later[0], shrink * earlier[1] + later[1])


def newton_inverse(system):
    bound = jnp.max(jnp.sum(jnp.abs(system), axis=-1), axis=-1)
    identity = jnp.eye(system.shape[-1], dtype=system.dtype)
    approx = identity / bound[..., None, None]
    for iteration in range(NEWTON):
        approx = product(approx, 2.0 * identity - product(system, approx))
    return approx


def solve_blocks(query_rows, key_t, beta_keys, start_gram, pre_gram, decay_row, mixing, ridge_col):
    identity = jnp.eye(query_rows.shape[-1], dtype=query_rows.dtype)
    system = start_gram + pre_gram + ridge_col * identity
    inverse = newton_inverse(system)
    solved = product(query_rows, inverse)
    for iteration in range(CORR - 1):
        attention_scores = mixing * product(solved, key_t)
        applied = (
            decay_row * product(solved, start_gram)
            + product(attention_scores, beta_keys)
            + ridge_col * solved
        )
        solved = solved + product(query_rows - applied, inverse)
    attention_scores = mixing * product(solved, key_t)
    return (solved, attention_scores)


def shift_down(field):
    return jnp.concatenate([jnp.zeros_like(field), field[:-1]], axis=0)


def on_device(queries, keys, values, log_forget, input_gate, ridge, gain, out_weight):
    tokens = queries.shape[0]
    count = tokens // C

    def blocks(field):
        return field.astype(jnp.float32).reshape(count, C, HEADS, DH).transpose(0, 2, 1, 3)

    def gate_blocks(field):
        return field.reshape(HEADS, count, C).transpose(1, 0, 2)

    query_all = unit_rows(blocks(queries))
    key_all = unit_rows(blocks(keys))
    value_all = blocks(values)
    forget_all = gate_blocks(log_forget)
    beta_all = gate_blocks(input_gate)
    running = jnp.cumsum(forget_all, axis=-1)
    block_decay = running[..., -1]
    decay_row = jnp.exp(running)[..., None]
    lower_mask = jnp.tril(jnp.ones((C, C), jnp.float32))
    mixing = lower_mask * jnp.exp(jnp.minimum(running[..., :, None] - running[..., None, :], 0.0))
    tail = (jnp.exp(block_decay[..., None] - running) * beta_all)[..., None]
    beta_col = beta_all[..., None]
    beta_keys = beta_col * key_all
    beta_values = beta_col * value_all
    key_t = jnp.swapaxes(key_all, -1, -2)
    block_grams = product(key_t, tail * key_all)
    block_states = product(key_t, tail * value_all)
    pre_grams = product(key_t, beta_keys)
    level_incl = jnp.cumsum(block_decay, axis=0)
    level_exclusive = level_incl - block_decay
    block_mask = jnp.tril(jnp.ones((count, count), jnp.float32))
    carry_weights = block_mask[:, :, None] * jnp.exp(
        jnp.minimum(level_incl[:, None, :] - level_incl[None, :, :], 0.0)
    )
    gram_incl = jnp.einsum("bch,chij->bhij", carry_weights, block_grams, precision=highest)
    state_incl = jnp.einsum("bch,chij->bhij", carry_weights, block_states, precision=highest)
    gram_local = shift_down(gram_incl)
    state_local = shift_down(state_incl)
    section_decay = level_incl[-1]
    gram_total = gram_incl[-1]
    state_total = state_incl[-1]
    carried = jnp.exp(level_exclusive)[..., None, None]
    ridge_col = ridge[None, :, None, None]
    zeros = jnp.zeros((HEADS, DH, DH), jnp.float32)
    zero_levels = jnp.zeros((HEADS,), jnp.float32)
    decay_before, gram_before = carried_in(
        (section_decay, gram_total), "seq", add_pairs, (zero_levels, zeros)
    )
    start_gram = carried * gram_before[None] + gram_local
    solved, attention_scores = solve_blocks(
        query_all, key_t, beta_keys, start_gram, pre_grams, decay_row, mixing, ridge_col
    )
    decay_again, state_before = prefix(
        (section_decay, state_total), "seq", add_pairs, (zero_levels, zeros)
    )
    start_state = carried * state_before[None] + state_local
    outputs = decay_row * product(solved, start_state) + product(attention_scores, beta_values)
    normed = outputs * lax.rsqrt(jnp.mean(outputs * outputs, axis=-1, keepdims=True) + 1e-06)
    normed = normed.transpose(0, 2, 1, 3).reshape(tokens, HEADS * DH) * gain
    normed = normed.astype(jnp.bfloat16)
    mixed = jnp.dot(
        normed,
        lax.all_gather(out_weight, "seq", axis=0, tiled=True),
        preferred_element_type=jnp.float32,
    )
    return mixed.astype(jnp.bfloat16)


def solution(mesh):
    placed = (
        P(("parts", "seq"), None),
        P(("parts", "seq"), None),
        P(("parts", "seq"), None),
        P(None, ("parts", "seq")),
        P(None, ("parts", "seq")),
        P(),
        P(),
        P("seq", None),
    )
    return jax.shard_map(
        on_device, mesh=mesh, in_specs=placed, out_specs=P(("parts", "seq"), None), check_vma=False
    )
```

profile of v0, /device:TPU:0, one launch (start us, length us, event | category | flops | bytes accessed | tf_op | source)
XLA Modules:
  0.0 202.5 jit_solution(14111731885373058151)
XLA Ops:
  6.5 1.1 copy.277
  7.7 1.1 copy.189
  8.9 1.0 reduce_window_sum.19
  10.8 1.9 fusion.14
  12.9 2.0 convolution_multiply_fusion.2
  15.7 23.1 %all-gather.1 = f32[16,8,1]{1,2,0:T(1,128)S(1)} all-gather(f32[1,8,1]{1,2,0:T(1,128)S(1)} %copy.278), channel_id=3, replica_groups=mesh['parts'=2,'seq'=16] {'seq'}, dimensions={0}, use_global_device_ids=true | all-gather | bytes 544 | tf_op jit(solution)/shard_map/all_gather | solution.py:36
  38.9 17.7 %all-gather.3 = bf16[16,8,1]{1,2,0:T(2,128)(2,1)S(1)} all-gather(bf16[1,8,1]{1,2,0:T(2,128)(2,1)S(1)} %convert_element_type.59), channel_id=5, replica_groups=mesh['parts'=2,'seq'=16] {'seq'}, dimensions={0}, use_global_device_ids=true | all-gather | bytes 272 | tf_op jit(solution)/shard_map/all_gather | solution.py:17
  56.9 9.2 %all-gather.10.cloned.1.call-done = bf16[128,128,128]{2,1,0:T(8,128)(2,1)} async-done(((bf16[8,128,128]{2,1,0:T(8,128)(2,1)}), bf16[128,128,128]{2,1,0:T(8,128)(2,1)}) %all-gather.10.cloned.1.call-update) | async-done | bytes 4194320 | tf_op jit(solution)/shard_map/all_gather | solution.py:17
  66.5 1.2 abs_reduce_fusion
  67.9 1.3 convolution_subtract_fusion.5
  69.2 1.1 fusion.37
  70.3 1.1 convolution_subtract_fusion.4
  72.0 1.1 convolution_subtract_fusion.3
  73.7 1.1 convolution_subtract_fusion.2
  75.4 1.1 convolution_subtract_fusion.1
  77.1 1.1 convolution_subtract_fusion
  78.9 1.2 fusion.30
  80.1 1.0 copy.214
  81.1 1.3 convolution_multiply_fusion.8
  83.1 2.2 %fusion.9 = f32[8,128,128]{1,2,0:T(8,128)S(1)} fusion(f32[8,128,128]{1,2,0:T(8,128)S(1)} %convolution_multiply_fusion.8, f32[8,128,128]{2,1,0:T(8,128)S(1)} %convolution_multiply_fusion.7, f32[8,128,128]{1,2,0:T(8,128)} %copy.214, f32[1,8,128,128]{2,3,1,0:T(8,128)S(1)} %bitcast.176, f32[1,8,128,128]{2,3,1,0:T(8,128)S(1)} %bitcast.168, f32[8]{0:T(128)S(1)} %copy-done.5, ...), kind=kOutput, calls=%fused_computation.38 | convolution fusion | flops 202244096 | bytes 3158048 | tf_op jit(solution)/shard_map/dot_general | solution.py:49
  85.3 1.0 convolution_add_fusion.5
  86.4 1.1 convolution_multiply_fusion.5
  88.1 1.2 fusion.11
  89.3 1.0 convolution_add_fusion.3
  91.0 1.1 convolution_multiply_fusion.3
  92.1 1.2 fusion.13
  93.3 1.0 convolution_add_fusion.1
  94.3 1.3 convolution_multiply_fusion
  95.7 45.4 %all-gather.12.cloned.1.call-done = f32[128,128,128]{2,1,0:T(8,128)} async-done(((f32[8,128,128]{2,1,0:T(8,128)}), f32[128,128,128]{2,1,0:T(8,128)}) %all-gather.12.cloned.1.call-update) | async-done | bytes 8388624 | tf_op jit(solution)/shard_map/all_gather | solution.py:36
  141.1 18.3 %while.27 = (s32[]{:T(128)}, f32[8,128,128]{2,1,0:T(8,128)S(1)}, s32[]{:T(128)}, f32[16,8]{1,0:T(8,128)S(1)}, f32[16,8,128,128]{3,2,1,0:T(8,128)}, /*index=5*/s32[]{:T(128)}, s32[]{:T(128)}) while((s32[]{:T(128)}, f32[8,128,128]{2,1,0:T(8,128)S(1)}, s32[]{:T(128)}, f32[16,8]{1,0:T(8,128)S(1)}, f32[16,8,128,128]{3,2,1,0:T(8,128)}, ...), condition=%wide.region_8.9_spmd.clone, body=%wide.region_7.8_spmd.clone.sunk | while | flops 524292 | bytes 1573065 | solution.py:45
  141.1 1.2 fusion.131
  142.4 1.2 fusion.131
  143.6 1.2 fusion.131
  144.8 1.2 fusion.131
  146.0 1.2 fusion.131
  147.2 1.2 fusion.131
  148.4 1.2 fusion.131
  149.7 1.2 fusion.131
  150.9 1.2 fusion.131
  152.1 1.2 fusion.131
  153.3 1.2 fusion.131
  154.5 1.2 fusion.131
  155.8 1.2 fusion.131
  157.0 1.2 fusion.131
  158.2 1.2 fusion.131
  160.3 1.2 multiply_reduce_fusion
  161.7 30.5 %all-gather.8.cloned.1.call-done = bf16[1024,2048]{1,0:T(8,128)(2,1)} async-done(((bf16[64,2048]{1,0:T(8,128)(2,1)}), bf16[1024,2048]{1,0:T(8,128)(2,1)}) %all-gather.8.cloned.1.call-update) | async-done | bytes 4194320 | tf_op jit(solution)/shard_map/all_gather | solution.py:153
  192.2 3.7 %convolution_convert_fusion = bf16[128,2048]{1,0:T(8,128)(2,1)} fusion(bf16[128,1024]{0,1:T(8,128)(2,1)S(1)} %fusion.15, bf16[1024,2048]{1,0:T(8,128)(2,1)} %all-gather.8.cloned.1.call-done), kind=kOutput, calls=%fused_computation.5 | convolution fusion | flops 537133056 | bytes 4980736 | tf_op jit(solution)/shard_map/dot_general | solution.py:151
  (68 shorter events, 9.2 us)
Async XLA Ops:
  6.5 6.2 %copy-start.3 = (bf16[128,1024]{1,0:T(8,128)(2,1)S(1)}, bf16[128,1024]{1,0:T(8,128)(2,1)}, u32[]{:S(2)}) copy-start(bf16[128,1024]{1,0:T(8,128)(2,1)} %param.14) | copy-start | bytes 786436
  6.5 59.5 %all-gather.10.cloned.1.call-start = ((), (), s32[]{:S(2)}) async-start(), calls=%async_computation.1 | async-start | bytes 4456448 | tf_op jit(solution)/shard_map/all_gather | solution.py:17
  12.7 128.4 %all-gather.12.cloned.1.call-start = ((), (), s32[]{:S(2)}) async-start(), calls=%async_computation.2 | async-start | bytes 8912896 | tf_op jit(solution)/shard_map/all_gather | solution.py:36
  12.9 53.1 %copy-start = (f32[128,1024]{0,1:T(8,128)}, f32[128,1024]{0,1:T(8,128)S(1)}, u32[]{:S(2)}) copy-start(f32[128,1024]{0,1:T(8,128)S(1)} %copy.276) | copy-start | bytes 1572868
  14.9 177.3 %all-gather.8.cloned.1.call-start = ((), (), s32[]{:S(2)}) async-start(), calls=%async_computation | async-start | bytes 4456448 | tf_op jit(solution)/shard_map/all_gather | solution.py:153
  56.8 9.7 %copy-start.4 = (f32[8,128]{1,0:T(8,128)S(1)}, f32[8,128]{1,0:T(8,128)}, u32[]{:S(2)}) copy-start(f32[8,128]{1,0:T(8,128)} %param.16) | copy-start | bytes 12292
  56.8 9.7 %copy-start.5 = (f32[8]{0:T(128)S(1)}, f32[8]{0:T(128)}, u32[]{:S(2)}) copy-start(f32[8]{0:T(128)} %param.17) | copy-start | bytes 100
  81.1 4.2 %copy-start.2 = (f32[8,128,128]{1,2,0:T(8,128)S(1)}, f32[8,128,128]{1,2,0:T(8,128)}, u32[]{:S(2)}) copy-start(f32[8,128,128]{1,2,0:T(8,128)} %copy.214) | copy-start | bytes 1572868
  141.1 19.2 %copy-start.1 = (f32[128,1024]{0,1:T(8,128)S(1)}, f32[128,1024]{0,1:T(8,128)}, u32[]{:S(2)}) copy-start(f32[128,1024]{0,1:T(8,128)} %copy-done) | copy-start | bytes 1572868
  159.4 2.2 %copy-start.6 = (f32[1024]{0:T(1024)S(1)}, f32[1024]{0:T(1024)}, u32[]{:S(2)}) copy-start(f32[1024]{0:T(1024)} %param.18) | copy-start | bytes 12292
Sparse Core Ops, SparseCore 0:
  12.8 53.1 all-gather.9
  68.2 72.8 all-gather.11
  143.2 48.9 all-gather.7
where the time goes:
time: 204 us; the launch traced here: 202 us
  waiting for transfers between devices  85.8 us (42%)
  blocking collectives  40.9 us (20%)
  matrix products  37.4 us (18%)
  other arithmetic  19.9 us (10%)
  between operations  13.5 us (7%)
  local copies, waits for them, and re-layouts  4.31 us (2%)
    all_gather x1, waiting for transfers between devices, prefix(): pieces = jax.tree.map(lambda part: lax.all_gather(part, axis), value)  45.4 us
    dot_general x31, matrix products, product(): return jnp.matmul(left, right, precision=highest)  33.7 us
    all_gather x1, waiting for transfers between devices, on_device(): lax.all_gather(out_weight, 'seq', axis=0, tiled=True)  30.5 us
    all_gather x1, blocking collectives, prefix(): pieces = jax.tree.map(lambda part: lax.all_gather(part, axis), value)  23.1 us
    all_gather x1, blocking collectives, carried_in(): lax.all_gather(a.astype(kind), axis)  17.7 us
    select_n x15, other arithmetic, step(): jnp.where(position < mine, new, old)  17.7 us
    all_gather x1, waiting for transfers between devices, carried_in(): lax.all_gather(a.astype(kind), axis)  9.19 us
  transfers between devices with their start and end apart: 3, of which 3 were waited for; matrix products, arithmetic and copies ran while one was open for 26% of the time, Pallas kernels for 0%

commit v1 on v0

--- a/solution.py
+++ b/solution.py
@@ -9,6 +9,22 @@
 NEWTON = 6
 CORR = 4
 highest = lax.Precision.HIGHEST
+
+
+def collect(x, axis, dim):
+    ways, here, step = (lax.axis_size(axis), lax.axis_index(axis), x.shape[dim])
+    shape = [n * ways if d == dim else n for d, n in enumerate(x.shape)]
+    full = lax.dynamic_update_slice_in_dim(jnp.zeros(shape, x.dtype), x, here * step, axis=dim)
+    going_up = going_down = x
+    for far in range(1, ways // 2 + 1):
+        going_up = lax.ppermute(going_up, axis, [(d, (d + 1) % ways) for d in range(ways)])
+        full = lax.dynamic_update_slice_in_dim(full, going_up, (here - far) % ways * step, axis=dim)
+        if 2 * far < ways:
+            going_down = lax.ppermute(going_down, axis, [(d, (d - 1) % ways) for d in range(ways)])
+            full = lax.dynamic_update_slice_in_dim(
+                full, going_down, (here + far) % ways * step, axis=dim
+            )
+    return full
 
 
 def carried_in(array, axis, join, neutral):
@@ -148,11 +164,7 @@
     normed = outputs * lax.rsqrt(jnp.mean(outputs * outputs, axis=-1, keepdims=True) + 1e-06)
     normed = normed.transpose(0, 2, 1, 3).reshape(tokens, HEADS * DH) * gain
     normed = normed.astype(jnp.bfloat16)
-    mixed = jnp.dot(
-        normed,
-        lax.all_gather(out_weight, "seq", axis=0, tiled=True),
-        preferred_element_type=jnp.float32,
-    )
+    mixed = jnp.dot(normed, collect(out_weight, "seq", 0), preferred_element_type=jnp.float32)
     return mixed.astype(jnp.bfloat16)
 
 

time: 204 us -> 216 us (1.059)
  the two profiles are of different devices: /device:TPU:0 before, /device:TPU:31 now
where the time goes in v1:
time: 216 us; the launch traced here: 214 us
  blocking collectives  38.8 us (18%)
  matrix products  37.6 us (17%)
  other arithmetic  36.8 us (17%)
  starting transfers between devices  34.1 us (16%)
  waiting for transfers between devices  33.2 us (15%)
  local copies, waits for them, and re-layouts  18.4 us (9%)
  between operations  14.2 us (7%)
    dot_general x31, matrix products, product(): return jnp.matmul(left, right, precision=highest)  33.9 us
    ppermute x8, starting transfers between devices, collect(): lax.ppermute(going_up, axis, [(d, (d + 1) % ways) for d in range(ways)])  33.8 us
    ppermute x7, waiting for transfers between devices, collect(): lax.ppermute(going_down, axis, [(d, (d - 1) % ways) for d in range(ways)])  22 us
    all_gather x1, blocking collectives, prefix(): pieces = jax.tree.map(lambda part: lax.all_gather(part, axis), value)  19.9 us
    all_gather x1, blocking collectives, carried_in(): lax.all_gather(a.astype(kind), axis)  18.8 us
    select_n x15, other arithmetic, step(): jnp.where(position < mine, new, old)  17.6 us
    add x15, other arithmetic, add_pairs(): return (earlier[0] + later[0], shrink * earlier[1] + later[1])  16.7 us
    ppermute x8, waiting for transfers between devices, collect(): lax.ppermute(going_up, axis, [(d, (d + 1) % ways) for d in range(ways)])  11.2 us
  transfers between devices with their start and end apart: 17, of which 10 were waited for; matrix products, arithmetic and copies ran while one was open for 29% of the time, Pallas kernels for 0%

profile of v1, /device:TPU:31, one launch (start us, length us, event | category | flops | bytes accessed | tf_op | source)
XLA Modules:
  0.0 214.2 jit_solution(13944910420782793269)
XLA Ops:
  10.8 1.9 fusion.14
  12.9 2.0 convolution_multiply_fusion.2
  16.1 18.8 %all-gather.3 = bf16[16,8,1]{1,2,0:T(2,128)(2,1)S(1)} all-gather(bf16[1,8,1]{1,2,0:T(2,128)(2,1)S(1)} %convert_element_type.59), channel_id=5, replica_groups=mesh['parts'=2,'seq'=16] {'seq'}, dimensions={0}, use_global_device_ids=true | all-gather | bytes 272 | tf_op jit(solution)/shard_map/all_gather | solution.py:33
  35.2 19.9 %all-gather.1 = f32[16,8,1]{1,2,0:T(1,128)S(1)} all-gather(f32[1,8,1]{1,2,0:T(1,128)S(1)} %copy.278), channel_id=3, replica_groups=mesh['parts'=2,'seq'=16] {'seq'}, dimensions={0}, use_global_device_ids=true | all-gather | bytes 544 | tf_op jit(solution)/shard_map/all_gather | solution.py:52
  55.2 2.5 %broadcast_in_dim.13 = bf16[1024,2048]{1,0:T(8,128)(2,1)} broadcast(bf16[]{:T(256)} %constant.156.clone.1), dimensions={} | broadcast | bytes 4194306 | tf_op jit(solution)/shard_map/broadcast_in_dim | solution.py:17
  58.3 2.8 %collective-permute-start.2 = (bf16[64,2048]{1,0:T(8,128)(2,1)S(1)}, bf16[64,2048]{1,0:T(8,128)(2,1)S(1)}, u32[]{:S(2)}, u32[]{:S(2)}) collective-permute-start(bf16[64,2048]{1,0:T(8,128)(2,1)S(1)} %collective-permute-done), channel_id=1, source_target_pairs={{0,1},{1,2},{2,3},{3,4},{4,5},{5,6},{6,7},{7,8},{8,9},{9,10},{10,1... | collective-permute-start | bytes 786440 | tf_op jit(solution)/shard_map/ppermute | solution.py:20
  62.6 1.8 collective-permute-done.2
  64.4 5.3 %collective-permute-start.4 = (bf16[64,2048]{1,0:T(8,128)(2,1)S(1)}, bf16[64,2048]{1,0:T(8,128)(2,1)S(1)}, u32[]{:S(2)}, u32[]{:S(2)}) collective-permute-start(bf16[64,2048]{1,0:T(8,128)(2,1)S(1)} %collective-permute-done.2), channel_id=1, source_target_pairs={{0,1},{1,2},{2,3},{3,4},{4,5},{5,6},{6,7},{7,8},{8,9},{9,10},{10,1... | collective-permute-start | bytes 786440 | tf_op jit(solution)/shard_map/ppermute | solution.py:20
  71.2 1.9 collective-permute-done.4
  73.0 5.3 %collective-permute-start.6 = (bf16[64,2048]{1,0:T(8,128)(2,1)S(1)}, bf16[64,2048]{1,0:T(8,128)(2,1)S(1)}, u32[]{:S(2)}, u32[]{:S(2)}) collective-permute-start(bf16[64,2048]{1,0:T(8,128)(2,1)S(1)} %collective-permute-done.4), channel_id=1, source_target_pairs={{0,1},{1,2},{2,3},{3,4},{4,5},{5,6},{6,7},{7,8},{8,9},{9,10},{10,1... | collective-permute-start | bytes 786440 | tf_op jit(solution)/shard_map/ppermute | solution.py:20
  78.3 5.3 %collective-permute-done.5 = bf16[64,2048]{1,0:T(8,128)(2,1)S(1)} collective-permute-done((bf16[64,2048]{1,0:T(8,128)(2,1)S(1)}, bf16[64,2048]{1,0:T(8,128)(2,1)S(1)}, u32[]{:S(2)}, u32[]{:S(2)}) %collective-permute-start.5) | collective-permute-done | bytes 262176 | tf_op jit(solution)/shard_map/ppermute | solution.py:23
  85.1 1.7 collective-permute-done.6
  86.8 5.1 %collective-permute-start.8 = (bf16[64,2048]{1,0:T(8,128)(2,1)S(1)}, bf16[64,2048]{1,0:T(8,128)(2,1)S(1)}, u32[]{:S(2)}, u32[]{:S(2)}) collective-permute-start(bf16[64,2048]{1,0:T(8,128)(2,1)S(1)} %collective-permute-done.6), channel_id=1, source_target_pairs={{0,1},{1,2},{2,3},{3,4},{4,5},{5,6},{6,7},{7,8},{8,9},{9,10},{10,1... | collective-permute-start | bytes 786440 | tf_op jit(solution)/shard_map/ppermute | solution.py:20
  91.9 5.5 %collective-permute-done.7 = bf16[64,2048]{1,0:T(8,128)(2,1)S(1)} collective-permute-done((bf16[64,2048]{1,0:T(8,128)(2,1)S(1)}, bf16[64,2048]{1,0:T(8,128)(2,1)S(1)}, u32[]{:S(2)}, u32[]{:S(2)}) %collective-permute-start.7) | collective-permute-done | bytes 262176 | tf_op jit(solution)/shard_map/ppermute | solution.py:23
  98.9 4.4 %collective-permute-start.10 = (bf16[64,2048]{1,0:T(8,128)(2,1)S(1)}, bf16[64,2048]{1,0:T(8,128)(2,1)S(1)}, u32[]{:S(2)}, u32[]{:S(2)}) collective-permute-start(bf16[64,2048]{1,0:T(8,128)(2,1)S(1)} %collective-permute-done.8), channel_id=1, source_target_pairs={{0,1},{1,2},{2,3},{3,4},{4,5},{5,6},{6,7},{7,8},{8,9},{9,10},{10,1... | collective-permute-start | bytes 786440 | tf_op jit(solution)/shard_map/ppermute | solution.py:20
  103.3 5.4 %collective-permute-done.9 = bf16[64,2048]{1,0:T(8,128)(2,1)S(1)} collective-permute-done((bf16[64,2048]{1,0:T(8,128)(2,1)S(1)}, bf16[64,2048]{1,0:T(8,128)(2,1)S(1)}, u32[]{:S(2)}, u32[]{:S(2)}) %collective-permute-start.9) | collective-permute-done | bytes 262176 | tf_op jit(solution)/shard_map/ppermute | solution.py:23
  110.2 2.0 collective-permute-done.10
  112.2 5.2 %collective-permute-start.12 = (bf16[64,2048]{1,0:T(8,128)(2,1)S(1)}, bf16[64,2048]{1,0:T(8,128)(2,1)S(1)}, u32[]{:S(2)}, u32[]{:S(2)}) collective-permute-start(bf16[64,2048]{1,0:T(8,128)(2,1)S(1)} %collective-permute-done.10), channel_id=1, source_target_pairs={{0,1},{1,2},{2,3},{3,4},{4,5},{5,6},{6,7},{7,8},{8,9},{9,10},{10,1... | collective-permute-start | bytes 786440 | tf_op jit(solution)/shard_map/ppermute | solution.py:20
  117.4 5.7 %collective-permute-done.11 = bf16[64,2048]{1,0:T(8,128)(2,1)S(1)} collective-permute-done((bf16[64,2048]{1,0:T(8,128)(2,1)S(1)}, bf16[64,2048]{1,0:T(8,128)(2,1)S(1)}, u32[]{:S(2)}, u32[]{:S(2)}) %collective-permute-start.11) | collective-permute-done | bytes 262176 | tf_op jit(solution)/shard_map/ppermute | solution.py:23
  124.5 2.0 collective-permute-done.12
  126.5 5.2 %collective-permute-start.14 = (bf16[64,2048]{1,0:T(8,128)(2,1)S(1)}, bf16[64,2048]{1,0:T(8,128)(2,1)S(1)}, u32[]{:S(2)}, u32[]{:S(2)}) collective-permute-start(bf16[64,2048]{1,0:T(8,128)(2,1)S(1)} %collective-permute-done.12), channel_id=1, source_target_pairs={{0,1},{1,2},{2,3},{3,4},{4,5},{5,6},{6,7},{7,8},{8,9},{9,10},{10,1... | collective-permute-start | bytes 786440 | tf_op jit(solution)/shard_map/ppermute | solution.py:20
  133.1 1.9 collective-permute-done.14
  135.7 17.5 %while.26 = (s32[]{:T(128)}, f32[8,128,128]{2,1,0:T(8,128)S(1)}, s32[]{:T(128)}, bf16[16,8]{1,0:T(8,128)(2,1)S(1)}, bf16[16,8,128,128]{3,2,1,0:T(8,128)(2,1)}, /*index=5*/s32[]{:T(128)}, s32[]{:T(128)}, s32[]{:T(128)}) while((s32[]{:T(128)}, f32[8,128,128]{2,1,0:T(8,128)S(1)}, s32[]{:T(128)}, bf16[16,8]{1,0:T(8,128)(2,1)S(1)}, ...), condition=%wide.region_4.5_spmd, body=%wide.region_3.4_spmd.sunk | while | flops 393229 | bytes 1310935 | solution.py:47
  153.5 1.2 abs_reduce_fusion
  154.9 1.3 convolution_subtract_fusion.5
  165.9 1.2 fusion.30
  168.2 1.3 convolution_multiply_fusion.8
  170.1 2.3 %fusion.9 = f32[8,128,128]{1,2,0:T(8,128)S(1)} fusion(f32[8,128,128]{1,2,0:T(8,128)S(1)} %convolution_multiply_fusion.8, f32[8,128,128]{2,1,0:T(8,128)S(1)} %convolution_multiply_fusion.7, f32[8,128,128]{1,2,0:T(8,128)} %copy.214, f32[1,8,128,128]{2,3,1,0:T(8,128)S(1)} %bitcast.176, f32[1,8,128,128]{2,3,1,0:T(8,128)S(1)} %bitcast.168, f32[8]{0:T(128)S(1)} %copy-done.6, ...), kind=kOutput, calls=%fused_computation.38 | convolution fusion | flops 202244096 | bytes 3158048 | tf_op jit(solution)/shard_map/dot_general | solution.py:65
  175.2 1.2 fusion.11
  179.3 1.2 fusion.13
  181.5 1.3 convolution_multiply_fusion
  182.9 18.3 %while.27 = (s32[]{:T(128)}, f32[8,128,128]{2,1,0:T(8,128)S(1)}, s32[]{:T(128)}, f32[16,8]{1,0:T(8,128)S(1)}, f32[16,8,128,128]{3,2,1,0:T(8,128)}, /*index=5*/s32[]{:T(128)}, s32[]{:T(128)}) while((s32[]{:T(128)}, f32[8,128,128]{2,1,0:T(8,128)S(1)}, s32[]{:T(128)}, f32[16,8]{1,0:T(8,128)S(1)}, f32[16,8,128,128]{3,2,1,0:T(8,128)}, ...), condition=%wide.region_8.9_spmd.clone, body=%wide.region_7.8_spmd.clone.sunk | while | flops 524292 | bytes 1573073 | solution.py:61
  182.9 1.2 fusion.131
  184.2 1.2 fusion.131
  185.4 1.2 fusion.131
  186.7 1.2 fusion.131
  187.9 1.2 fusion.131
  189.1 1.2 fusion.131
  190.3 1.2 fusion.131
  191.5 1.2 fusion.131
  194.0 1.2 fusion.131
  195.2 1.2 fusion.131
  196.4 1.2 fusion.131
  197.6 1.2 fusion.131
  198.8 1.2 fusion.131
  200.1 1.2 fusion.131
  202.1 1.2 multiply_reduce_fusion
  203.6 3.7 %convolution_convert_fusion = bf16[128,2048]{1,0:T(8,128)(2,1)} fusion(bf16[128,1024]{0,1:T(8,128)(2,1)S(1)} %fusion.15, bf16[1024,2048]{1,0:T(8,128)(2,1)} %constant_dynamic-update-slice_fusion), kind=kOutput, calls=%fused_computation.5 | convolution fusion | flops 537133056 | bytes 4980736 | tf_op jit(solution)/shard_map/dot_general | solution.py:167
  (144 shorter events, 54.7 us)
Async XLA Ops:
  6.5 6.2 %copy-start.3 = (bf16[128,1024]{1,0:T(8,128)(2,1)S(1)}, bf16[128,1024]{1,0:T(8,128)(2,1)}, u32[]{:S(2)}) copy-start(bf16[128,1024]{1,0:T(8,128)(2,1)} %param.14) | copy-start | bytes 786436
  6.5 8.4 %copy-start.4 = (bf16[64,2048]{1,0:T(8,128)(2,1)S(1)}, bf16[64,2048]{1,0:T(8,128)(2,1)}, u32[]{:S(2)}) copy-start(bf16[64,2048]{1,0:T(8,128)(2,1)} %param.19) | copy-start | bytes 786436
  6.5 129.1 %all-gather.7.cloned.1.call-start = ((), (), s32[]{:S(2)}) async-start(), calls=%async_computation | async-start | bytes 4456448 | tf_op jit(solution)/shard_map/all_gather | solution.py:33
  12.7 170.2 %all-gather.9.cloned.1.call-start = ((), (), s32[]{:S(2)}) async-start(), calls=%async_computation.1 | async-start | bytes 8912896 | tf_op jit(solution)/shard_map/all_gather | solution.py:52
  12.9 49.7 %copy-start = (f32[128,1024]{0,1:T(8,128)}, f32[128,1024]{0,1:T(8,128)S(1)}, u32[]{:S(2)}) copy-start(f32[128,1024]{0,1:T(8,128)S(1)} %copy.276) | copy-start | bytes 1572868
  15.0 43.3 %collective-permute-start = (bf16[64,2048]{1,0:T(8,128)(2,1)S(1)}, bf16[64,2048]{1,0:T(8,128)(2,1)S(1)}, u32[]{:S(2)}, u32[]{:S(2)}) collective-permute-start(bf16[64,2048]{1,0:T(8,128)(2,1)S(1)} %copy-done.4), channel_id=1, source_target_pairs={{0,1},{1,2},{2,3},{3,4},{4,5},{5,6},{6,7},{7,8},{8,9},{9,10},{10,1... | collective-permute-start | bytes 786440 | tf_op jit(solution)/shard_map/ppermute | solution.py:20
  15.5 45.6 %collective-permute-start.1 = (bf16[64,2048]{1,0:T(8,128)(2,1)S(1)}, bf16[64,2048]{1,0:T(8,128)(2,1)S(1)}, u32[]{:S(2)}, u32[]{:S(2)}) collective-permute-start(bf16[64,2048]{1,0:T(8,128)(2,1)S(1)} %copy-done.4), channel_id=1, source_target_pairs={{0,15},{1,0},{2,1},{3,2},{4,3},{5,4},{6,5},{7,6},{8,7},{9,8},{10,9... | collective-permute-start | bytes 786440 | tf_op jit(solution)/shard_map/ppermute | solution.py:23
  58.3 6.1 %collective-permute-start.2 = (bf16[64,2048]{1,0:T(8,128)(2,1)S(1)}, bf16[64,2048]{1,0:T(8,128)(2,1)S(1)}, u32[]{:S(2)}, u32[]{:S(2)}) collective-permute-start(bf16[64,2048]{1,0:T(8,128)(2,1)S(1)} %collective-permute-done), channel_id=1, source_target_pairs={{0,1},{1,2},{2,3},{3,4},{4,5},{5,6},{6,7},{7,8},{8,9},{9,10},{10,1... | collective-permute-start | bytes 786440 | tf_op jit(solution)/shard_map/ppermute | solution.py:20
  61.1 8.6 %collective-permute-start.3 = (bf16[64,2048]{1,0:T(8,128)(2,1)S(1)}, bf16[64,2048]{1,0:T(8,128)(2,1)S(1)}, u32[]{:S(2)}, u32[]{:S(2)}) collective-permute-start(bf16[64,2048]{1,0:T(8,128)(2,1)S(1)} %collective-permute-done.1), channel_id=1, source_target_pairs={{0,15},{1,0},{2,1},{3,2},{4,3},{5,4},{6,5},{7,6},{8,7},{9,8},{10,9... | collective-permute-start | bytes 786440 | tf_op jit(solution)/shard_map/ppermute | solution.py:23
  64.4 8.6 %collective-permute-start.4 = (bf16[64,2048]{1,0:T(8,128)(2,1)S(1)}, bf16[64,2048]{1,0:T(8,128)(2,1)S(1)}, u32[]{:S(2)}, u32[]{:S(2)}) collective-permute-start(bf16[64,2048]{1,0:T(8,128)(2,1)S(1)} %collective-permute-done.2), channel_id=1, source_target_pairs={{0,1},{1,2},{2,3},{3,4},{4,5},{5,6},{6,7},{7,8},{8,9},{9,10},{10,1... | collective-permute-start | bytes 786440 | tf_op jit(solution)/shard_map/ppermute | solution.py:20
  69.7 13.9 %collective-permute-start.5 = (bf16[64,2048]{1,0:T(8,128)(2,1)S(1)}, bf16[64,2048]{1,0:T(8,128)(2,1)S(1)}, u32[]{:S(2)}, u32[]{:S(2)}) collective-permute-start(bf16[64,2048]{1,0:T(8,128)(2,1)S(1)} %collective-permute-done.3), channel_id=1, source_target_pairs={{0,15},{1,0},{2,1},{3,2},{4,3},{5,4},{6,5},{7,6},{8,7},{9,8},{10,9... | collective-permute-start | bytes 786440 | tf_op jit(solution)/shard_map/ppermute | solution.py:23
  73.0 13.7 %collective-permute-start.6 = (bf16[64,2048]{1,0:T(8,128)(2,1)S(1)}, bf16[64,2048]{1,0:T(8,128)(2,1)S(1)}, u32[]{:S(2)}, u32[]{:S(2)}) collective-permute-start(bf16[64,2048]{1,0:T(8,128)(2,1)S(1)} %collective-permute-done.4), channel_id=1, source_target_pairs={{0,1},{1,2},{2,3},{3,4},{4,5},{5,6},{6,7},{7,8},{8,9},{9,10},{10,1... | collective-permute-start | bytes 786440 | tf_op jit(solution)/shard_map/ppermute | solution.py:20
  83.6 13.8 %collective-permute-start.7 = (bf16[64,2048]{1,0:T(8,128)(2,1)S(1)}, bf16[64,2048]{1,0:T(8,128)(2,1)S(1)}, u32[]{:S(2)}, u32[]{:S(2)}) collective-permute-start(bf16[64,2048]{1,0:T(8,128)(2,1)S(1)} %collective-permute-done.5), channel_id=1, source_target_pairs={{0,15},{1,0},{2,1},{3,2},{4,3},{5,4},{6,5},{7,6},{8,7},{9,8},{10,9... | collective-permute-start | bytes 786440 | tf_op jit(solution)/shard_map/ppermute | solution.py:23
  86.8 12.1 %collective-permute-start.8 = (bf16[64,2048]{1,0:T(8,128)(2,1)S(1)}, bf16[64,2048]{1,0:T(8,128)(2,1)S(1)}, u32[]{:S(2)}, u32[]{:S(2)}) collective-permute-start(bf16[64,2048]{1,0:T(8,128)(2,1)S(1)} %collective-permute-done.6), channel_id=1, source_target_pairs={{0,1},{1,2},{2,3},{3,4},{4,5},{5,6},{6,7},{7,8},{8,9},{9,10},{10,1... | collective-permute-start | bytes 786440 | tf_op jit(solution)/shard_map/ppermute | solution.py:20
  97.4 11.3 %collective-permute-start.9 = (bf16[64,2048]{1,0:T(8,128)(2,1)S(1)}, bf16[64,2048]{1,0:T(8,128)(2,1)S(1)}, u32[]{:S(2)}, u32[]{:S(2)}) collective-permute-start(bf16[64,2048]{1,0:T(8,128)(2,1)S(1)} %collective-permute-done.7), channel_id=1, source_target_pairs={{0,15},{1,0},{2,1},{3,2},{4,3},{5,4},{6,5},{7,6},{8,7},{9,8},{10,9... | collective-permute-start | bytes 786440 | tf_op jit(solution)/shard_map/ppermute | solution.py:23
  98.9 13.3 %collective-permute-start.10 = (bf16[64,2048]{1,0:T(8,128)(2,1)S(1)}, bf16[64,2048]{1,0:T(8,128)(2,1)S(1)}, u32[]{:S(2)}, u32[]{:S(2)}) collective-permute-start(bf16[64,2048]{1,0:T(8,128)(2,1)S(1)} %collective-permute-done.8), channel_id=1, source_target_pairs={{0,1},{1,2},{2,3},{3,4},{4,5},{5,6},{6,7},{7,8},{8,9},{9,10},{10,1... | collective-permute-start | bytes 786440 | tf_op jit(solution)/shard_map/ppermute | solution.py:20
  108.8 14.3 %collective-permute-start.11 = (bf16[64,2048]{1,0:T(8,128)(2,1)S(1)}, bf16[64,2048]{1,0:T(8,128)(2,1)S(1)}, u32[]{:S(2)}, u32[]{:S(2)}) collective-permute-start(bf16[64,2048]{1,0:T(8,128)(2,1)S(1)} %collective-permute-done.9), channel_id=1, source_target_pairs={{0,15},{1,0},{2,1},{3,2},{4,3},{5,4},{6,5},{7,6},{8,7},{9,8},{10,9... | collective-permute-start | bytes 786440 | tf_op jit(solution)/shard_map/ppermute | solution.py:23
  112.2 14.2 %collective-permute-start.12 = (bf16[64,2048]{1,0:T(8,128)(2,1)S(1)}, bf16[64,2048]{1,0:T(8,128)(2,1)S(1)}, u32[]{:S(2)}, u32[]{:S(2)}) collective-permute-start(bf16[64,2048]{1,0:T(8,128)(2,1)S(1)} %collective-permute-done.10), channel_id=1, source_target_pairs={{0,1},{1,2},{2,3},{3,4},{4,5},{5,6},{6,7},{7,8},{8,9},{9,10},{10,1... | collective-permute-start | bytes 786440 | tf_op jit(solution)/shard_map/ppermute | solution.py:20
  123.1 9.3 %collective-permute-start.13 = (bf16[64,2048]{1,0:T(8,128)(2,1)S(1)}, bf16[64,2048]{1,0:T(8,128)(2,1)S(1)}, u32[]{:S(2)}, u32[]{:S(2)}) collective-permute-start(bf16[64,2048]{1,0:T(8,128)(2,1)S(1)} %collective-permute-done.11), channel_id=1, source_target_pairs={{0,15},{1,0},{2,1},{3,2},{4,3},{5,4},{6,5},{7,6},{8,7},{9,8},{10,9... | collective-permute-start | bytes 786440 | tf_op jit(solution)/shard_map/ppermute | solution.py:23
  126.5 8.5 %collective-permute-start.14 = (bf16[64,2048]{1,0:T(8,128)(2,1)S(1)}, bf16[64,2048]{1,0:T(8,128)(2,1)S(1)}, u32[]{:S(2)}, u32[]{:S(2)}) collective-permute-start(bf16[64,2048]{1,0:T(8,128)(2,1)S(1)} %collective-permute-done.12), channel_id=1, source_target_pairs={{0,1},{1,2},{2,3},{3,4},{4,5},{5,6},{6,7},{7,8},{8,9},{9,10},{10,1... | collective-permute-start | bytes 786440 | tf_op jit(solution)/shard_map/ppermute | solution.py:20
  135.7 17.8 %copy-start.5 = (f32[8,128]{1,0:T(8,128)S(1)}, f32[8,128]{1,0:T(8,128)}, u32[]{:S(2)}) copy-start(f32[8,128]{1,0:T(8,128)} %param.16) | copy-start | bytes 12292
  135.7 17.8 %copy-start.6 = (f32[8]{0:T(128)S(1)}, f32[8]{0:T(128)}, u32[]{:S(2)}) copy-start(f32[8]{0:T(128)} %param.17) | copy-start | bytes 100
  168.2 4.3 %copy-start.2 = (f32[8,128,128]{1,2,0:T(8,128)S(1)}, f32[8,128,128]{1,2,0:T(8,128)}, u32[]{:S(2)}) copy-start(f32[8,128,128]{1,2,0:T(8,128)} %copy.214) | copy-start | bytes 1572868
  182.9 19.2 %copy-start.1 = (f32[128,1024]{0,1:T(8,128)S(1)}, f32[128,1024]{0,1:T(8,128)}, u32[]{:S(2)}) copy-start(f32[128,1024]{0,1:T(8,128)} %copy-done) | copy-start | bytes 1572868
  201.2 2.2 %copy-start.7 = (f32[1024]{0:T(1024)S(1)}, f32[1024]{0:T(1024)}, u32[]{:S(2)}) copy-start(f32[1024]{0:T(1024)} %param.18) | copy-start | bytes 12292
Sparse Core Ops, SparseCore 0:
  12.8 49.5 all-gather.6
  64.6 86.9 all-gather.8
